TPU v7x, 768 devices: a whole 4x8x12 slice. The times are simulated.
768 devices in a mesh: dp: 8 (over x, core), row: 32 (over y, z_hi), col: 3 (over z_lo).
Axes of the slice: x: 4, y: 8, z: 12 (z_hi: 4, z_lo: 3; z = z_hi * 3 + z_lo), core: 2. Of those that a mesh axis runs over, the one named last changes fastest.
Arguments:
- grad_parts: bfloat16 [8, 1, 4096, 3, 4096], P('dp', None, 'row', 'col'), may hold values from -128 to 128
- weights: bfloat16 [1, 4096, 3, 4096], P(None, 'row', 'col', 'dp'), may hold values from -0.09375 to 0.09375
- row_old: float32 [1, 4096], P(None, 'row'), may hold values from 0.5 to 2
- col_old: float32 [1, 3, 4096], P(None, 'col', 'dp'), may hold values from 0.5 to 32
- step_rates: float32 [1], replicated, may hold values from 0.1 to 0.3
Outputs:
- new_weights: bfloat16 [1, 4096, 3, 4096], P(None, 'row', 'col', 'dp')
- row_moment: float32 [1, 4096], P(None, 'row')
- col_moment: float32 [1, 3, 4096], P(None, 'col', 'dp')
All inputs are finite; a program needn't handle non-finite values.
Results may differ from a plain program's by a relative error of at most 0.001.
Values sent between devices are 32-bit elements; how exact they have to be, the bound alone decides.
A program may use at most 32 MiB of HBM per device.

v0:
```python
import jax
import jax.numpy as jnp
from jax import lax
from jax.sharding import PartitionSpec as P

D = 4096
QKV = 12288


eps_floor = 1e-30


def per_device(grad_parts, weights, row_old, col_old, step_rates):
    partial_value = grad_parts[0].astype(jnp.float32)
    gradient = lax.psum_scatter(partial_value, "dp", scatter_dimension=3, tiled=True)
    squares = gradient * gradient + eps_floor
    row_sum = lax.psum(jnp.sum(squares, axis=(2, 3)), ("dp", "col"))
    row_moment = 0.8 * row_old + 0.2 * row_sum / QKV
    local_col = jnp.sum(squares, axis=1)
    col_sum = lax.psum(local_col, "row")
    col_moment = 0.8 * col_old + 0.2 * col_sum / D
    second = row_moment[:, :, None, None] * col_moment[:, None, :, :]
    update = gradient / jnp.sqrt(second)
    update_total = lax.psum(jnp.sum(update * update, axis=(1, 2, 3)), ("dp", "row", "col"))
    clip_factor = 1.0 / jnp.maximum(1.0, jnp.sqrt(update_total / (D * QKV)) / 0.2)
    step_size = (step_rates * clip_factor)[:, None, None, None]
    new_weights = (weights.astype(jnp.float32) - step_size * update).astype(jnp.bfloat16)
    return (new_weights, row_moment, col_moment)


def solution(mesh):
    in_specs = (
        P("dp", None, "row", "col", None),
        P(None, "row", "col", "dp"),
        P(None, "row"),
        P(None, "col", "dp"),
        P(),
    )
    out_specs = (P(None, "row", "col", "dp"), P(None, "row"), P(None, "col", "dp"))
    return jax.shard_map(
        per_device, mesh=mesh, in_specs=in_specs, out_specs=out_specs, check_vma=False
    )
```

profile of v0, /device:TPU:1, one launch (start us, length us, event | category | flops | bytes accessed | tf_op | source)
XLA Modules:
  0.0 321.2 jit_solution(9149867175600365244)
XLA Ops:
  7.2 0.0 copy-start.2
  7.2 0.0 copy-start.4
  7.2 0.0 reduce-scatter.2.cloned.1.call-start
  7.2 2.8 bitcast_convert_fusion
  10.0 0.0 copy-start
  10.0 0.0 reduce-scatter.2.cloned.1.call-update
  10.7 48.7 %reduce-scatter.2.cloned.1.call-done = f32[1,128,1,512]{3,1,2,0:T(8,128)} async-done(((f32[1,128,1,4096]{3,1,2,0:T(8,128)}), f32[1,128,1,512]{3,1,2,0:T(8,128)}) %reduce-scatter.2.cloned.1.call-update) | async-done | bytes 262160 | tf_op jit(solution)/shard_map/reduce_scatter | solution.py:15
  59.4 1.1 fusion.1
  60.5 76.5 %psum.22 = f32[1,1,512]{2,1,0:T(1,128)S(1)} all-reduce(f32[1,1,512]{2,1,0:T(1,128)S(1)} %bitcast.11), channel_id=1, replica_groups=mesh['dp'=8,'row'=32,'col'=3] {'row'}, use_global_device_ids=true, to_apply=%region_4.0 | all-reduce | flops 512 | bytes 4096 | tf_op jit(solution)/shard_map/psum | solution.py:20
  136.9 62.4 %psum.21 = f32[1,128]{1,0:T(1,128)S(1)} all-reduce(f32[1,128]{1,0:T(1,128)S(1)} %bitcast.14), channel_id=1, replica_groups=mesh['dp'=8,'row'=32,'col'=3] {'dp','col'}, use_global_device_ids=true, to_apply=%region_2.0 | all-reduce | flops 128 | bytes 1024 | tf_op jit(solution)/shard_map/psum | solution.py:17
  199.4 0.0 copy-done.2
  199.4 0.0 copy-done.4
  199.4 0.0 copy-start.1
  199.4 0.0 copy-start.3
  199.4 1.7 multiply_reduce_fusion
  201.1 110.7 %psum.23 = f32[1]{0:T(128)} all-reduce(f32[1]{0:T(128)} %bitcast.5), channel_id=1, replica_groups=mesh['dp'=8,'row'=32,'col'=3] {'dp','row','col'}, use_global_device_ids=true, to_apply=%region_6.0 | all-reduce | flops 1 | bytes 8 | tf_op jit(solution)/shard_map/psum | solution.py:24
  312.6 0.0 copy-done
  312.6 1.7 subtract_convert_fusion
  314.3 0.0 copy-done.1
  314.3 0.0 copy-done.3
  (2 shorter events, 0.0 us)
Async XLA Ops:
  7.2 192.2 %copy-start.2 = (f32[1,1,512]{2,1,0:T(1,128)S(1)}, f32[1,1,512]{2,1,0:T(1,128)}, u32[]{:S(2)}) copy-start(f32[1,1,512]{2,1,0:T(1,128)} %param.8) | copy-start | bytes 6148
  7.2 192.2 %copy-start.4 = (f32[1,128]{1,0:T(1,128)S(1)}, f32[1,128]{1,0:T(1,128)}, u32[]{:S(2)}) copy-start(f32[1,128]{1,0:T(1,128)} %param.7) | copy-start | bytes 1540
  7.2 52.2 %reduce-scatter.2.cloned.1.call-start = ((), (), s32[]{:S(2)}) async-start(), calls=%async_computation.1 | async-start | bytes 2359296 | tf_op jit(solution)/shard_map/reduce_scatter | solution.py:15
  10.0 302.6 %copy-start = (bf16[1,128,1,512]{3,1,2,0:T(8,128)(2,1)S(1)}, bf16[1,128,1,512]{3,1,2,0:T(8,128)(2,1)}, u32[]{:S(2)}) copy-start(bf16[1,128,1,512]{3,1,2,0:T(8,128)(2,1)} %param.6) | copy-start | bytes 393220
  199.4 114.9 %copy-start.1 = (f32[1,1,512]{2,1,0:T(1,128)}, f32[1,1,512]{2,1,0:T(1,128)S(1)}, u32[]{:S(2)}) copy-start(f32[1,1,512]{2,1,0:T(1,128)S(1)} %multiply_add_fusion.1) | copy-start | bytes 6148
  199.4 114.9 %copy-start.3 = (f32[1,128]{1,0:T(1,128)}, f32[1,128]{1,0:T(1,128)S(1)}, u32[]{:S(2)}) copy-start(f32[1,128]{1,0:T(1,128)S(1)} %multiply_add_fusion.2) | copy-start | bytes 1540
Sparse Core Ops, SparseCore 0:
  11.1 48.1 reduce-scatter.1
where the time goes:
time: 322 us; the launch traced here: 321 us
  blocking collectives  250 us (78%)
  waiting for transfers between devices  48.7 us (15%)
  between operations  15.5 us (5%)
  other arithmetic  7.3 us (2%)
    psum x1, blocking collectives, per_device(): lax.psum(jnp.sum(update * update, axis=(1, 2, 3)), ('dp', 'row', 'col'))  111 us
    psum x1, blocking collectives, per_device(): col_sum = lax.psum(local_col, 'row')  76.5 us
    psum x1, blocking collectives, per_device(): row_sum = lax.psum(jnp.sum(squares, axis=(2, 3)), ('dp', 'col'))  62.4 us
    reduce_scatter x1, waiting for transfers between devices, per_device(): lax.psum_scatter(partial_value, 'dp', scatter_dimension=3, tiled=True)  48.7 us
  transfers between devices with their start and end apart: 1, of which 1 were waited for; matrix products, arithmetic and copies ran while one was open for 0% of the time, Pallas kernels for 0%

commit v1 on v0

v1 whole, which is shorter than its diff:
```python
import functools

import jax
import jax.numpy as jnp
from jax import lax
from jax.experimental import pallas as pl
from jax.experimental.pallas import tpu as pltpu
from jax.sharding import PartitionSpec as P

D = 4096
QKV = 12288
EPS = 1e-30
MESH = pl.DeviceIdType.MESH
CHUNKS = 4


def kernel(n_dp, n_row, n_col, g_hbm, w_ref, ro_ref, co_ref, sr_ref, ow_ref, orow_ref, ocol_ref,
           gb, snd, prt, b1, q1, b2, q2, gf, rowbuf, colbuf, totbuf, cold,
           load_sem, core_send, core_recv, s1_send, s1_recv, s2_send, s2_recv, ar_send, ar_recv):
    rows = gb.shape[0]
    cols = gf.shape[1]
    half = cols // 2
    lanes = 128
    groups = cols // lanes
    rc = rows // CHUNKS
    nx = n_dp // 2
    n_flat = n_dp * n_col

    dp = lax.axis_index("dp")
    row = lax.axis_index("row")
    col = lax.axis_index("col")
    x = lax.div(dp, 2)
    core = lax.rem(dp, 2)
    me = dp * n_col + col
    partner = dp + 1 - 2 * core

    def dev(d, r, c):
        return {"dp": d, "row": r, "col": c}

    def load(k):
        rs = pl.ds(k * rc, rc)
        return pltpu.make_async_copy(g_hbm.at[rs], gb.at[rs], load_sem.at[k])

    for k in range(CHUNKS):
        load(k).start()

    flat_peers = []
    for dc in range(n_col):
        for dd in range(n_dp):
            if dc or dd:
                flat_peers.append((lax.rem(dp + dd, n_dp), lax.rem(col + dc, n_col)))
    row_peers = [lax.rem(row + r, n_row) for r in range(1, n_row)]

    barrier = pltpu.get_barrier_semaphore()
    for d, c in flat_peers:
        pl.semaphore_signal(barrier, inc=1, device_id=dev(d, row, c), device_id_type=MESH)
    for r in row_peers:
        pl.semaphore_signal(barrier, inc=1, device_id=dev(dp, r, col), device_id_type=MESH)

    def block(k, rel, who):
        j = 2 * lax.rem(x + rel, nx) + who
        start = pl.multiple_of(j * cols, cols)
        return gb[pl.ds(k * rc, rc), pl.ds(start, cols)].astype(jnp.float32)

    def core_copy(k):
        return pltpu.make_async_remote_copy(
            src_ref=snd.at[k], dst_ref=prt.at[k], send_sem=core_send.at[k], recv_sem=core_recv.at[k],
            device_id=dev(partner, row, col), device_id_type=MESH)

    right = 2 * lax.rem(x + 1, nx) + core
    left = 2 * lax.rem(x + nx - 1, nx) + core

    def hop(buf, out, k, side, send_sem, recv_sem):
        return pltpu.make_async_remote_copy(
            src_ref=buf.at[k, side], dst_ref=out.at[k, side], send_sem=send_sem.at[k, side],
            recv_sem=recv_sem.at[k, side],
            device_id=dev(right if side == 0 else left, row, col), device_id_type=MESH)

    for k in range(CHUNKS):
        load(k).wait()
        for rel in range(nx):
            snd[k, rel] = block(k, rel, 1 - core)
        if k == 0:
            pl.semaphore_wait(barrier, len(flat_peers) + len(row_peers))
        core_copy(k).start()

    def stage1(k):
        core_copy(k).wait_recv()
        far = block(k, 2, core) + prt[k, 2]
        b1[k, 0] = far[:, :half]
        b1[k, 1] = far[:, half:]
        for side in range(2):
            hop(b1, q1, k, side, s1_send, s1_recv).start()

    def stage2(k):
        for side, rel in ((0, 1), (1, nx - 1)):
            hop(b1, q1, k, side, s1_send, s1_recv).wait_recv()
            near = block(k, rel, core) + prt[k, rel]
            lo, hi = near[:, :half], near[:, half:]
            if side == 0:
                lo = lo + q1[k, 0]
            else:
                hi = hi + q1[k, 1]
            b2[k, side, :, :half] = lo
            b2[k, side, :, half:] = hi
            hop(b2, q2, k, side, s2_send, s2_recv).start()

    def finish(k):
        own = block(k, 0, core) + prt[k, 0]
        for side in range(2):
            hop(b2, q2, k, side, s2_send, s2_recv).wait_recv()
            own = own + q2[k, side]
        gf[pl.ds(k * rc, rc), :] = own

    for k in range(CHUNKS + 2):
        if k < CHUNKS:
            stage1(k)
        if 0 <= k - 1 < CHUNKS:
            stage2(k - 1)
        if k - 2 >= 0:
            finish(k - 2)

    def exchange_flat(buf, i):
        for d, c in flat_peers:
            pltpu.make_async_remote_copy(
                src_ref=buf.at[me], dst_ref=buf.at[me], send_sem=ar_send.at[i], recv_sem=ar_recv.at[i],
                device_id=dev(d, row, c), device_id_type=MESH).start()

    def all_of(buf, n, i):
        return pltpu.make_async_remote_copy(
            src_ref=buf.at[pl.ds(0, n)], dst_ref=buf.at[pl.ds(0, n)], send_sem=ar_send.at[i], recv_sem=ar_recv.at[i],
            device_id=dev(partner, row, col), device_id_type=MESH)

    acc = jnp.zeros((rows, lanes), jnp.float32)
    for q in range(groups):
        v = gf[:, q * lanes:(q + 1) * lanes]
        sq = v * v + EPS
        acc = acc + sq
        colbuf[row, q:q + 1, :] = jnp.sum(sq, axis=0, keepdims=True)
        cold[q:q + 1, :] = co_ref[:, q * lanes:(q + 1) * lanes]
    rowbuf[me] = jnp.sum(acc.T, axis=0, keepdims=True)
    exchange_flat(rowbuf, 0)
    all_of(rowbuf, n_flat - 1, 0).wait_recv()
    row_sum = jnp.sum(rowbuf[...], axis=0)
    row_moment = 0.8 * ro_ref[...] + 0.2 * row_sum / QKV
    orow_ref[...] = row_moment
    scale = jnp.broadcast_to(lax.rsqrt(row_moment), (lanes, rows)).T

    for q in range(groups):
        h = gf[:, q * lanes:(q + 1) * lanes] * scale
        gf[:, q * lanes:(q + 1) * lanes] = h
        colbuf[row, groups + q:groups + q + 1, :] = jnp.sum(h * h, axis=0, keepdims=True)
    for r in row_peers:
        pltpu.make_async_remote_copy(
            src_ref=colbuf.at[row], dst_ref=colbuf.at[row], send_sem=ar_send.at[1], recv_sem=ar_recv.at[1],
            device_id=dev(dp, r, col), device_id_type=MESH).start()
    all_of(colbuf, n_row - 1, 1).wait_recv()
    both = jnp.sum(colbuf[...], axis=0)
    col_moment = 0.8 * cold[...] + 0.2 * both[:groups] / D
    part = both[groups:] / col_moment
    totbuf[me] = jnp.sum(part, axis=0, keepdims=True)
    exchange_flat(totbuf, 2)
    inv = lax.rsqrt(col_moment)
    for q in range(groups):
        ocol_ref[:, q * lanes:(q + 1) * lanes] = col_moment[q:q + 1]
        gf[:, q * lanes:(q + 1) * lanes] = gf[:, q * lanes:(q + 1) * lanes] * inv[q:q + 1]
    all_of(totbuf, n_flat - 1, 2).wait_recv()
    total = jnp.sum(jnp.sum(totbuf[...], axis=0), axis=1, keepdims=True)
    clip = 1.0 / jnp.maximum(1.0, jnp.sqrt(total / (D * QKV)) / 0.2)
    step = sr_ref[0] * clip
    ow_ref[...] = (w_ref[...].astype(jnp.float32) - step * gf[...]).astype(jnp.bfloat16)

    for k in range(CHUNKS):
        core_copy(k).wait_send()
        for side in range(2):
            hop(b1, q1, k, side, s1_send, s1_recv).wait_send()
            hop(b2, q2, k, side, s2_send, s2_recv).wait_send()
    all_of(rowbuf, n_flat - 1, 0).wait_send()
    all_of(colbuf, n_row - 1, 1).wait_send()
    all_of(totbuf, n_flat - 1, 2).wait_send()


def solution(mesh):
    n_dp, n_row, n_col = (mesh.shape[a] for a in ("dp", "row", "col"))

    def per_device(grad_parts, weights, row_old, col_old, step_rates):
        rows, width = grad_parts.shape[2], grad_parts.shape[4]
        cols = weights.shape[3]
        nx = n_dp // 2
        rc = rows // CHUNKS
        f32 = jnp.float32
        vmem = pl.BlockSpec(memory_space=pltpu.VMEM)
        dma = pltpu.SemaphoreType.DMA
        new_w, row_moment, col_moment = pl.pallas_call(
            functools.partial(kernel, n_dp, n_row, n_col),
            out_shape=(
                jax.ShapeDtypeStruct((rows, cols), jnp.bfloat16),
                jax.ShapeDtypeStruct((1, rows), f32),
                jax.ShapeDtypeStruct((1, cols), f32),
            ),
            in_specs=[pl.BlockSpec(memory_space=pl.ANY), vmem, vmem, vmem, pl.BlockSpec(memory_space=pltpu.SMEM)],
            out_specs=(vmem, vmem, vmem),
            scratch_shapes=[
                pltpu.VMEM((rows, width), jnp.bfloat16),
                pltpu.VMEM((CHUNKS, nx, rc, cols), f32),
                pltpu.VMEM((CHUNKS, nx, rc, cols), f32),
                pltpu.VMEM((CHUNKS, 2, rc, cols // 2), f32),
                pltpu.VMEM((CHUNKS, 2, rc, cols // 2), f32),
                pltpu.VMEM((CHUNKS, 2, rc, cols), f32),
                pltpu.VMEM((CHUNKS, 2, rc, cols), f32),
                pltpu.VMEM((rows, cols), f32),
                pltpu.VMEM((n_dp * n_col, 1, 128), f32),
                pltpu.VMEM((n_row, 8, 128), f32),
                pltpu.VMEM((n_dp * n_col, 1, 128), f32),
                pltpu.VMEM((4, 128), f32),
                dma((CHUNKS,)),
                dma((CHUNKS,)), dma((CHUNKS,)),
                dma((CHUNKS, 2)), dma((CHUNKS, 2)),
                dma((CHUNKS, 2)), dma((CHUNKS, 2)),
                dma((3,)), dma((3,)),
            ],
            compiler_params=pltpu.CompilerParams(collective_id=0, has_side_effects=True, vmem_limit_bytes=24 << 20),
        )(grad_parts.reshape(rows, width), weights.reshape(rows, cols), row_old, col_old.reshape(1, cols), step_rates)
        return new_w.reshape(weights.shape), row_moment, col_moment.reshape(col_old.shape)

    in_specs = (
        P("dp", None, "row", "col", None),
        P(None, "row", "col", "dp"),
        P(None, "row"),
        P(None, "col", "dp"),
        P(),
    )
    out_specs = (P(None, "row", "col", "dp"), P(None, "row"), P(None, "col", "dp"))
    return jax.shard_map(per_device, mesh=mesh, in_specs=in_specs, out_specs=out_specs, check_vma=False)
```

time: 322 us -> 62 us (0.19)
  blocking collectives: 250 us -> 0 us
  Pallas kernels: 0 us -> 55.9 us
  waiting for transfers between devices: 48.7 us -> 0 us
  between operations: 15.5 us -> 1.31 us
  other arithmetic: 7.3 us -> 0 us
  local copies, waits for them, and re-layouts: 0.03 us -> 4.54 us
    psum x3 -> x0, blocking collectives: 250 us -> none  [the longest x1 111 us: per_device(): lax.psum(jnp.sum(update * update, axis=(1, 2, 3)), ('dp', 'row', 'col'))]
    pallas_call x0 -> x1, Pallas kernels: none -> 55.9 us  [per_device(): pl.pallas_call(functools.partial(kernel, n_dp, n_row, n_col), out_shape=(...]
    reduce_scatter x1 -> x0, waiting for transfers between devices: 48.7 us -> none  [per_device(): lax.psum_scatter(partial_value, 'dp', scatter_dimension=3, tiled=True)]
    convert_element_type x2 -> x0, other arithmetic: 4.52 us -> none  [the longest x1 2.79 us: per_device(): partial_value = grad_parts[0].astype(jnp.float32)]
    unnamed x10 -> x11, local copies, waits for them, and re-layouts: 0.03 us -> 4.54 us
  transfers between devices with their start and end apart: 1 -> 0, of which waited for: 1 -> 0; matrix products, arithmetic and copies ran while one was open for 0% -> 0% of each run, Pallas kernels for 0% -> 0%
where the time goes in v1:
time: 62 us; the launch traced here: 61.8 us
  Pallas kernels  55.9 us (90%)
  local copies, waits for them, and re-layouts  4.54 us (7%)
  between operations  1.31 us (2%)
    pallas_call x1, Pallas kernels, per_device(): pl.pallas_call(functools.partial(kernel, n_dp, n_row, n_col), out_shape=(...  55.9 us
    unnamed x11, local copies, waits for them, and re-layouts  4.54 us

profile of v1, /device:TPU:1, one launch (start us, length us, event | category | flops | bytes accessed | tf_op | source)
XLA Modules:
  0.0 61.8 jit_solution(834599985973527815)
XLA Ops:
  1.3 0.0 copy-start.2
  1.3 0.0 copy-start.3
  1.3 0.7 %copy-done.2 = f32[1,1,512]{2,1,0:T(1,128)S(1)} copy-done((f32[1,1,512]{2,1,0:T(1,128)S(1)}, f32[1,1,512]{2,1,0:T(1,128)}, u32[]{:S(2)}) %copy-start.2) | copy-done | bytes 2072
  2.0 0.0 copy-done.3
  2.0 0.0 copy-start
  2.0 1.2 %copy-done = bf16[1,1,128,1,4096]{4,2,3,1,0:T(8,128)(2,1)S(1)} copy-done((bf16[1,1,128,1,4096]{4,2,3,1,0:T(8,128)(2,1)S(1)}, bf16[1,1,128,1,4096]{4,2,3,1,0:T(8,128)(2,1)}, u32[]{:S(2)}) %copy-start) | copy-done | bytes 1048600
  3.2 0.0 copy-start.1
  3.2 0.9 %copy-done.1 = bf16[1,128,1,512]{3,1,2,0:T(8,128)(2,1)S(1)} copy-done((bf16[1,128,1,512]{3,1,2,0:T(8,128)(2,1)S(1)}, bf16[1,128,1,512]{3,1,2,0:T(8,128)(2,1)}, u32[]{:S(2)}) %copy-start.1) | copy-done | bytes 131096
  4.1 55.9 %shard_map.76 = (bf16[128,512]{1,0:T(8,128)(2,1)S(1)}, f32[1,128]{1,0:T(1,128)S(1)}, f32[1,512]{1,0:T(1,128)S(1)}) custom-call(bf16[128,4096]{1,0:T(8,128)(2,1)S(1)} %bitcast.5, bf16[128,512]{1,0:T(8,128)(2,1)S(1)} %bitcast.7, f32[1,128]{1,0:T(1,128)S(1)} %copy-done.3, f32[1,512]{1,0:T(1,128)S(1)} %bitcast.8, f32[1]{0:T(128)S(6)} %copy.11.sr_ref), custom_call_target="tpu_custom_call" | custom-call | tf_op jit(solution)/shard_map/pallas_call | solution.py:194
  60.0 0.7 %copy.12 = bf16[1,128,1,512]{3,1,2,0:T(8,128)(2,1)} copy(bf16[1,128,1,512]{3,1,2,0:T(8,128)(2,1)S(1)} %bitcast.6) | data formatting | bytes 262144
  60.7 0.5 copy.13
  61.2 0.6 copy.14
Async XLA Ops:
  1.3 0.7 %copy-start.2 = (f32[1,1,512]{2,1,0:T(1,128)S(1)}, f32[1,1,512]{2,1,0:T(1,128)}, u32[]{:S(2)}) copy-start(f32[1,1,512]{2,1,0:T(1,128)} %param.8) | copy-start | bytes 6148
  1.3 0.7 %copy-start.3 = (f32[1,128]{1,0:T(1,128)S(1)}, f32[1,128]{1,0:T(1,128)}, u32[]{:S(2)}) copy-start(f32[1,128]{1,0:T(1,128)} %ro_ref.1) | copy-start | bytes 1540
  2.0 1.2 %copy-start = (bf16[1,1,128,1,4096]{4,2,3,1,0:T(8,128)(2,1)S(1)}, bf16[1,1,128,1,4096]{4,2,3,1,0:T(8,128)(2,1)}, u32[]{:S(2)}) copy-start(bf16[1,1,128,1,4096]{4,2,3,1,0:T(8,128)(2,1)} %param.5) | copy-start | bytes 3145732
  3.2 0.9 %copy-start.1 = (bf16[1,128,1,512]{3,1,2,0:T(8,128)(2,1)S(1)}, bf16[1,128,1,512]{3,1,2,0:T(8,128)(2,1)}, u32[]{:S(2)}) copy-start(bf16[1,128,1,512]{3,1,2,0:T(8,128)(2,1)} %param.6) | copy-start | bytes 393220

commit v2 on v0

v2 whole, which is shorter than its diff:
```python
import functools

import jax
import jax.numpy as jnp
from jax import lax
from jax.experimental import pallas as pl
from jax.experimental.pallas import tpu as pltpu
from jax.sharding import PartitionSpec as P

D = 4096
QKV = 12288
EPS = 1e-30
MESH = pl.DeviceIdType.MESH
CHUNKS = 4
LANES = 128
NX, NCORE, NY, NZHI, NZLO = 4, 2, 8, 4, 3
NZ = NZHI * NZLO


def kernel(g_hbm, w_hbm, ro_hbm, co_hbm, sr_hbm, ow_ref, orow_ref, ocol_ref,
           gb, snd, prt, b1, q1, b2, q2, gf, wv, ro, co, sr, rowbuf, colbuf, totbuf,
           load_sem, misc_sem, core_send, core_recv, s1_send, s1_recv, s2_send, s2_recv, ar_send, ar_recv, met):
    rows, cols = gf.shape
    half = cols // 2
    groups = cols // LANES
    rc = rows // CHUNKS
    n_flat = NX * NCORE * NZLO
    n_row = NY * NZHI

    dp = lax.axis_index("dp")
    row = lax.axis_index("row")
    col = lax.axis_index("col")
    x, core = lax.div(dp, NCORE), lax.rem(dp, NCORE)
    y, zhi = lax.div(row, NZHI), lax.rem(row, NZHI)
    z = zhi * NZLO + col
    me = dp * NZLO + col

    def at(dx=0, dc=0, dy=0, dz=0):
        zz = lax.rem(z + dz + NZ, NZ)
        return {
            "dp": lax.rem(x + dx + NX, NX) * NCORE + lax.rem(core + dc, NCORE),
            "row": lax.rem(y + dy + NY, NY) * NZHI + lax.div(zz, NZLO),
            "col": lax.rem(zz, NZLO),
        }

    def flat_at(dx, dc, k):
        return {"dp": lax.rem(x + dx, NX) * NCORE + lax.rem(core + dc, NCORE), "row": row, "col": lax.rem(col + k, NZLO)}

    def row_at(dy, dz):
        return {"dp": dp, "row": lax.rem(y + dy, NY) * NZHI + lax.rem(zhi + dz, NZHI), "col": col}

    flat_peers = [flat_at(dx, dc, k) for dx in (2, 1, 3, 0) for k in (1, 2, 0) for dc in (1, 0) if dx or dc or k]
    row_peers = [row_at(dy, dz) for dy, dz in sorted(
        ((dy, dz) for dy in range(NY) for dz in range(NZHI) if dy or dz),
        key=lambda p: -(min(p[0], NY - p[0]) + 3 * min(p[1], NZHI - p[1])))]

    near = [at(dc=1), at(dx=1), at(dx=-1), at(dy=1), at(dy=-1), at(dz=1), at(dz=-1)]
    steps = [
        near,
        [at(dc=1), at(dx=2), at(dy=2), at(dy=-2), at(dz=2), at(dz=-2)],
        [at(dc=1), at(dz=3), at(dz=-3)],
        [at(dz=3), at(dz=-3)],
    ]

    barrier = pltpu.get_barrier_semaphore()
    for d in near:
        pl.semaphore_signal(barrier, inc=1, device_id=d, device_id_type=MESH)

    def tell(s):
        for d in steps[s]:
            pl.semaphore_signal(met.at[s], inc=1, device_id=d, device_id_type=MESH)

    def hear(s):
        pl.semaphore_wait(met.at[s], len(steps[s]))

    def load(rel, who):
        j = lax.rem(x + rel, NX) * NCORE + (core if who == 0 else 1 - core)
        i = 2 * rel + who
        return pltpu.make_async_copy(
            g_hbm.at[:, pl.ds(pl.multiple_of(j * cols, cols), cols)], gb.at[i], load_sem.at[i])

    order = (2, 1, 3, 0)
    for rel in order:
        for who in (1, 0):
            load(rel, who).start()
    misc = [pltpu.make_async_copy(a, b, misc_sem.at[i])
            for i, (a, b) in enumerate(((w_hbm, wv), (ro_hbm, ro), (co_hbm, co), (sr_hbm, sr)))]
    for m in misc:
        m.start()

    def part(rel, who, rs):
        return gb[2 * rel + who, rs, :].astype(jnp.float32)

    def chunk(k):
        return pl.ds(k * rc, rc)

    def core_copy(i):
        if i < CHUNKS:
            src, dst = snd.at[2, chunk(i)], prt.at[2, chunk(i)]
        else:
            src, dst = snd.at[order[i - CHUNKS + 1]], prt.at[order[i - CHUNKS + 1]]
        return pltpu.make_async_remote_copy(
            src_ref=src, dst_ref=dst, send_sem=core_send.at[i], recv_sem=core_recv.at[i],
            device_id=at(dc=1), device_id_type=MESH)

    n_core = CHUNKS + 3

    def hop(buf, out, k, side, send_sem, recv_sem):
        return pltpu.make_async_remote_copy(
            src_ref=buf.at[k, side], dst_ref=out.at[k, side], send_sem=send_sem.at[k, side],
            recv_sem=recv_sem.at[k, side],
            device_id=at(dx=1 if side == 0 else -1), device_id_type=MESH)

    whole = pl.ds(0, rows)
    for n, rel in enumerate(order):
        load(rel, 1).wait()
        snd[rel] = part(rel, 1, whole)
        if n == 0:
            pl.semaphore_wait(barrier, len(near))
            for i in range(CHUNKS):
                core_copy(i).start()
        else:
            core_copy(CHUNKS + n - 1).start()
    tell(0)

    load(2, 0).wait()
    for k in range(CHUNKS):
        core_copy(k).wait_recv()
        far = part(2, 0, chunk(k)) + prt[2, chunk(k), :]
        b1[k, 0] = far[:, :half]
        b1[k, 1] = far[:, half:]
        for side in range(2):
            hop(b1, q1, k, side, s1_send, s1_recv).start()
    hear(0)
    tell(1)
    load(1, 0).wait()
    load(3, 0).wait()
    core_copy(CHUNKS).wait_recv()
    core_copy(CHUNKS + 1).wait_recv()
    for k in range(CHUNKS):
        for side, rel in ((0, 1), (1, 3)):
            near_sum = part(rel, 0, chunk(k)) + prt[rel, chunk(k), :]
            lo, hi = near_sum[:, :half], near_sum[:, half:]
            hop(b1, q1, k, side, s1_send, s1_recv).wait_recv()
            if side == 0:
                lo = lo + q1[k, 0]
            else:
                hi = hi + q1[k, 1]
            b2[k, side, :, :half] = lo
            b2[k, side, :, half:] = hi
            hop(b2, q2, k, side, s2_send, s2_recv).start()
    hear(1)
    tell(2)
    load(0, 0).wait()
    core_copy(CHUNKS + 2).wait_recv()
    for m in misc:
        m.wait()
    for k in range(CHUNKS):
        own = part(0, 0, chunk(k)) + prt[0, chunk(k), :]
        for side in range(2):
            hop(b2, q2, k, side, s2_send, s2_recv).wait_recv()
            own = own + q2[k, side]
        gf[chunk(k), :] = own

    def exchange(buf, slot, peers, i):
        for d in peers:
            pltpu.make_async_remote_copy(
                src_ref=buf.at[slot], dst_ref=buf.at[slot], send_sem=ar_send.at[i], recv_sem=ar_recv.at[i],
                device_id=d, device_id_type=MESH).start()

    def all_of(buf, n, i):
        return pltpu.make_async_remote_copy(
            src_ref=buf.at[pl.ds(0, n)], dst_ref=buf.at[pl.ds(0, n)], send_sem=ar_send.at[i], recv_sem=ar_recv.at[i],
            device_id=at(dc=1), device_id_type=MESH)

    def lane(q):
        return slice(q * LANES, (q + 1) * LANES)

    acc = jnp.zeros((rows, LANES), jnp.float32)
    for q in range(groups):
        v = gf[:, lane(q)]
        acc = acc + (v * v + EPS)
    rowbuf[me] = jnp.sum(acc.T, axis=0, keepdims=True)
    hear(2)
    exchange(rowbuf, me, flat_peers, 0)
    tell(3)
    for q in range(groups):
        v = gf[:, lane(q)]
        colbuf[row, q:q + 1, :] = jnp.sum(v * v + EPS, axis=0, keepdims=True)
    all_of(rowbuf, n_flat - 1, 0).wait_recv()
    row_sum = jnp.sum(rowbuf[...], axis=0)
    row_moment = 0.8 * ro[...] + 0.2 * row_sum / QKV
    orow_ref[...] = row_moment
    scale = jnp.broadcast_to(lax.rsqrt(row_moment), (LANES, rows)).T

    for q in range(groups):
        h = gf[:, lane(q)] * scale
        gf[:, lane(q)] = h
        colbuf[row, groups + q:groups + q + 1, :] = jnp.sum(h * h, axis=0, keepdims=True)
    hear(3)
    exchange(colbuf, row, row_peers, 1)
    all_of(colbuf, n_row - 1, 1).wait_recv()
    both = jnp.sum(colbuf[...], axis=0)
    total_part = jnp.zeros((1, LANES), jnp.float32)
    for q in range(groups):
        col_moment = 0.8 * co[:, lane(q)] + 0.2 * both[q:q + 1] / D
        ocol_ref[:, lane(q)] = col_moment
        total_part = total_part + both[groups + q:groups + q + 1] / col_moment
    totbuf[me] = total_part
    exchange(totbuf, me, flat_peers, 2)
    for q in range(groups):
        gf[:, lane(q)] = gf[:, lane(q)] * lax.rsqrt(ocol_ref[:, lane(q)])
    all_of(totbuf, n_flat - 1, 2).wait_recv()
    total = jnp.sum(jnp.sum(totbuf[...], axis=0), axis=1, keepdims=True)
    clip = 1.0 / jnp.maximum(1.0, jnp.sqrt(total / (D * QKV)) / 0.2)
    step = sr[...] * clip
    ow_ref[...] = (wv[...].astype(jnp.float32) - step * gf[...]).astype(jnp.bfloat16)

    for i in range(n_core):
        core_copy(i).wait_send()
    for k in range(CHUNKS):
        for side in range(2):
            hop(b1, q1, k, side, s1_send, s1_recv).wait_send()
            hop(b2, q2, k, side, s2_send, s2_recv).wait_send()
    all_of(rowbuf, n_flat - 1, 0).wait_send()
    all_of(colbuf, n_row - 1, 1).wait_send()
    all_of(totbuf, n_flat - 1, 2).wait_send()


def solution(mesh):
    def per_device(grad_parts, weights, row_old, col_old, step_rates):
        rows, width = grad_parts.shape[2], grad_parts.shape[4]
        cols = weights.shape[3]
        rc = rows // CHUNKS
        f32 = jnp.float32
        vmem = pl.BlockSpec(memory_space=pltpu.VMEM)
        hbm = pl.BlockSpec(memory_space=pltpu.HBM)
        dma = pltpu.SemaphoreType.DMA
        shapes = (
            jax.ShapeDtypeStruct((rows, cols), jnp.bfloat16),
            jax.ShapeDtypeStruct((1, rows), f32),
            jax.ShapeDtypeStruct((1, cols), f32),
        )
        new_w, row_moment, col_moment = pl.pallas_call(
            kernel,
            out_shape=shapes,
            in_specs=[hbm] * 5,
            out_specs=(vmem,) * 3,
            scratch_shapes=[
                pltpu.VMEM((2 * NX, rows, cols), jnp.bfloat16),
                pltpu.VMEM((NX, rows, cols), f32),
                pltpu.VMEM((NX, rows, cols), f32),
                pltpu.VMEM((CHUNKS, 2, rc, cols // 2), f32),
                pltpu.VMEM((CHUNKS, 2, rc, cols // 2), f32),
                pltpu.VMEM((CHUNKS, 2, rc, cols), f32),
                pltpu.VMEM((CHUNKS, 2, rc, cols), f32),
                pltpu.VMEM((rows, cols), f32),
                pltpu.VMEM((rows, cols), jnp.bfloat16),
                pltpu.VMEM((1, rows), f32),
                pltpu.VMEM((1, cols), f32),
                pltpu.VMEM((1, 1), f32),
                pltpu.VMEM((NX * NCORE * NZLO, 1, LANES), f32),
                pltpu.VMEM((NY * NZHI, 8, LANES), f32),
                pltpu.VMEM((NX * NCORE * NZLO, 1, LANES), f32),
                dma((2 * NX,)), dma((4,)),
                dma((CHUNKS + 3,)), dma((CHUNKS + 3,)),
                dma((CHUNKS, 2)), dma((CHUNKS, 2)),
                dma((CHUNKS, 2)), dma((CHUNKS, 2)),
                dma((3,)), dma((3,)),
                pltpu.SemaphoreType.REGULAR((4,)),
            ],
            compiler_params=pltpu.CompilerParams(collective_id=0, has_side_effects=True, vmem_limit_bytes=63 << 20),
        )(grad_parts.reshape(rows, width), weights.reshape(rows, cols), row_old, col_old.reshape(1, cols), step_rates.reshape(1, 1))
        return new_w.reshape(weights.shape), row_moment, col_moment.reshape(col_old.shape)

    in_specs = (
        P("dp", None, "row", "col", None),
        P(None, "row", "col", "dp"),
        P(None, "row"),
        P(None, "col", "dp"),
        P(),
    )
    out_specs = (P(None, "row", "col", "dp"), P(None, "row"), P(None, "col", "dp"))
    return jax.shard_map(per_device, mesh=mesh, in_specs=in_specs, out_specs=out_specs, check_vma=False)
```

time: 322 us -> 52.9 us (0.16)
  blocking collectives: 250 us -> 0 us
  Pallas kernels: 0 us -> 48.7 us
  waiting for transfers between devices: 48.7 us -> 0 us
  between operations: 15.5 us -> 1.3 us
  other arithmetic: 7.3 us -> 0 us
    psum x3 -> x0, blocking collectives: 250 us -> none  [the longest x1 111 us: per_device(): lax.psum(jnp.sum(update * update, axis=(1, 2, 3)), ('dp', 'row', 'col'))]
    pallas_call x0 -> x1, Pallas kernels: none -> 48.7 us  [per_device(): pl.pallas_call(kernel, out_shape=shapes, in_specs=[hbm] * 5, out_specs=(v...]
    reduce_scatter x1 -> x0, waiting for transfers between devices: 48.7 us -> none  [per_device(): lax.psum_scatter(partial_value, 'dp', scatter_dimension=3, tiled=True)]
    convert_element_type x2 -> x0, other arithmetic: 4.52 us -> none  [the longest x1 2.79 us: per_device(): partial_value = grad_parts[0].astype(jnp.float32)]
  transfers between devices with their start and end apart: 1 -> 0, of which waited for: 1 -> 0; matrix products, arithmetic and copies ran while one was open for 0% -> 0% of each run, Pallas kernels for 0% -> 0%
where the time goes in v2:
time: 52.9 us; the launch traced here: 52.7 us
  Pallas kernels  48.7 us (92%)
  local copies, waits for them, and re-layouts  2.67 us (5%)
  between operations  1.3 us (2%)
    pallas_call x1, Pallas kernels, per_device(): pl.pallas_call(kernel, out_shape=shapes, in_specs=[hbm] * 5, out_specs=(v...  48.7 us
    unnamed x7, local copies, waits for them, and re-layouts  2.67 us

profile of v2, /device:TPU:1, one launch (start us, length us, event | category | flops | bytes accessed | tf_op | source)
XLA Modules:
  0.0 52.7 jit_solution(11065143460832222513)
XLA Ops:
  1.3 48.7 %shard_map.76 = (bf16[128,512]{1,0:T(8,128)(2,1)}, f32[1,128]{1,0:T(1,128)}, f32[1,512]{1,0:T(1,128)}) custom-call(bf16[128,4096]{1,0:T(8,128)(2,1)} %bitcast.7, bf16[128,512]{1,0:T(8,128)(2,1)} %bitcast.9, f32[1,128]{1,0:T(1,128)} %ro_hbm.1, f32[1,512]{1,0:T(1,128)} %bitcast.10, f32[1,1]{1,0:T(1,128)} %bitcast.6.sr_hbm), custom_call_target="tpu_custom_call" | custom-call | tf_op jit(solution)/shard_map/pallas_call | solution.py:244
  50.0 0.0 copy-start.1
  50.0 0.0 copy-start
  50.1 1.6 %copy.12 = bf16[1,128,1,512]{3,1,2,0:T(8,128)(2,1)} copy(bf16[1,128,1,512]{3,1,2,0:T(8,128)(2,1)} %bitcast.8) | data formatting | bytes 262144
  51.6 0.0 copy-done.1
  51.6 0.5 copy.13
  52.1 0.0 copy-done
  52.1 0.6 %copy.14 = f32[1,1,512]{2,1,0:T(1,128)} copy(f32[1,1,512]{2,1,0:T(1,128)S(1)} %bitcast.11) | data formatting | bytes 4096
Async XLA Ops:
  50.0 1.6 %copy-start.1 = (f32[1,128]{1,0:T(1,128)S(1)}, f32[1,128]{1,0:T(1,128)}, u32[]{:S(2)}) copy-start(f32[1,128]{1,0:T(1,128)} %get-tuple-element.13) | copy-start | bytes 1540
  50.0 2.1 %copy-start = (f32[1,512]{1,0:T(1,128)S(1)}, f32[1,512]{1,0:T(1,128)}, u32[]{:S(2)}) copy-start(f32[1,512]{1,0:T(1,128)} %get-tuple-element.8) | copy-start | bytes 6148

commit v3 on v2

--- a/solution.py
+++ b/solution.py
@@ -17,9 +17,9 @@
 NZ = NZHI * NZLO
 
 
-def kernel(g_hbm, w_hbm, ro_hbm, co_hbm, sr_hbm, ow_ref, orow_ref, ocol_ref,
-           gb, snd, prt, b1, q1, b2, q2, gf, wv, ro, co, sr, rowbuf, colbuf, totbuf,
-           load_sem, misc_sem, core_send, core_recv, s1_send, s1_recv, s2_send, s2_recv, ar_send, ar_recv, met):
+def kernel(g_hbm, ro_hbm, co_hbm, sr_hbm, gf, step_ref, orow_ref, ocol_ref,
+           gb, snd, prt, fs, fr, js, jr, ds, dr, ro, co, sr, rowbuf, colbuf, totbuf,
+           load_sem, misc_sem, core_send, core_recv, f_send, f_recv, j_send, j_recv, d_send, d_recv, ar_send, ar_recv, met):
     rows, cols = gf.shape
     half = cols // 2
     groups = cols // LANES
@@ -84,12 +84,13 @@
         for who in (1, 0):
             load(rel, who).start()
     misc = [pltpu.make_async_copy(a, b, misc_sem.at[i])
-            for i, (a, b) in enumerate(((w_hbm, wv), (ro_hbm, ro), (co_hbm, co), (sr_hbm, sr)))]
+            for i, (a, b) in enumerate(((ro_hbm, ro), (co_hbm, co), (sr_hbm, sr)))]
     for m in misc:
         m.start()
 
-    def part(rel, who, rs):
-        return gb[2 * rel + who, rs, :].astype(jnp.float32)
+    def part(rel, who, rs, side=None):
+        cs = slice(None) if side is None else halves[side]
+        return gb[2 * rel + who, rs, cs].astype(jnp.float32)
 
     def chunk(k):
         return pl.ds(k * rc, rc)
@@ -105,10 +106,11 @@
 
     n_core = CHUNKS + 3
 
-    def hop(buf, out, k, side, send_sem, recv_sem):
+    halves = (pl.ds(0, half), pl.ds(half, half))
+
+    def hop(buf, out, idx, side, send_sem, recv_sem):
         return pltpu.make_async_remote_copy(
-            src_ref=buf.at[k, side], dst_ref=out.at[k, side], send_sem=send_sem.at[k, side],
-            recv_sem=recv_sem.at[k, side],
+            src_ref=buf.at[idx], dst_ref=out.at[idx], send_sem=send_sem.at[idx], recv_sem=recv_sem.at[idx],
             device_id=at(dx=1 if side == 0 else -1), device_id_type=MESH)
 
     whole = pl.ds(0, rows)
@@ -127,40 +129,36 @@
     for k in range(CHUNKS):
         core_copy(k).wait_recv()
         far = part(2, 0, chunk(k)) + prt[2, chunk(k), :]
-        b1[k, 0] = far[:, :half]
-        b1[k, 1] = far[:, half:]
         for side in range(2):
-            hop(b1, q1, k, side, s1_send, s1_recv).start()
+            fs[k, side] = far[:, side * half:(side + 1) * half]
+            hop(fs, fr, (k, side), side, f_send, f_recv).start()
     hear(0)
     tell(1)
-    load(1, 0).wait()
-    load(3, 0).wait()
-    core_copy(CHUNKS).wait_recv()
-    core_copy(CHUNKS + 1).wait_recv()
+    for side, rel in ((0, 1), (1, 3)):
+        load(rel, 0).wait()
+        core_copy(CHUNKS + side).wait_recv()
+        js[side] = part(rel, 0, whole, 1 - side) + prt[rel, :, halves[1 - side]]
+        hop(js, jr, (side,), side, j_send, j_recv).start()
     for k in range(CHUNKS):
         for side, rel in ((0, 1), (1, 3)):
-            near_sum = part(rel, 0, chunk(k)) + prt[rel, chunk(k), :]
-            lo, hi = near_sum[:, :half], near_sum[:, half:]
-            hop(b1, q1, k, side, s1_send, s1_recv).wait_recv()
-            if side == 0:
-                lo = lo + q1[k, 0]
-            else:
-                hi = hi + q1[k, 1]
-            b2[k, side, :, :half] = lo
-            b2[k, side, :, half:] = hi
-            hop(b2, q2, k, side, s2_send, s2_recv).start()
+            near_sum = part(rel, 0, chunk(k), side) + prt[rel, chunk(k), halves[side]]
+            hop(fs, fr, (k, side), side, f_send, f_recv).wait_recv()
+            ds[k, side] = near_sum + fr[k, side]
+            hop(ds, dr, (k, side), side, d_send, d_recv).start()
     hear(1)
     tell(2)
     load(0, 0).wait()
     core_copy(CHUNKS + 2).wait_recv()
     for m in misc:
         m.wait()
+    for side in range(2):
+        hop(js, jr, (side,), side, j_send, j_recv).wait_recv()
+    for side in range(2):
+        gf[:, halves[side]] = part(0, 0, whole, side) + prt[0, :, halves[side]] + jr[1 - side]
     for k in range(CHUNKS):
-        own = part(0, 0, chunk(k)) + prt[0, chunk(k), :]
         for side in range(2):
-            hop(b2, q2, k, side, s2_send, s2_recv).wait_recv()
-            own = own + q2[k, side]
-        gf[chunk(k), :] = own
+            hop(ds, dr, (k, side), side, d_send, d_recv).wait_recv()
+            gf[chunk(k), halves[side]] = gf[chunk(k), halves[side]] + dr[k, side]
 
     def exchange(buf, slot, peers, i):
         for d in peers:
@@ -213,18 +211,33 @@
     all_of(totbuf, n_flat - 1, 2).wait_recv()
     total = jnp.sum(jnp.sum(totbuf[...], axis=0), axis=1, keepdims=True)
     clip = 1.0 / jnp.maximum(1.0, jnp.sqrt(total / (D * QKV)) / 0.2)
-    step = sr[...] * clip
-    ow_ref[...] = (wv[...].astype(jnp.float32) - step * gf[...]).astype(jnp.bfloat16)
+    step_ref[...] = jnp.broadcast_to(sr[...] * clip, step_ref.shape)
 
     for i in range(n_core):
         core_copy(i).wait_send()
     for k in range(CHUNKS):
         for side in range(2):
-            hop(b1, q1, k, side, s1_send, s1_recv).wait_send()
-            hop(b2, q2, k, side, s2_send, s2_recv).wait_send()
+            hop(fs, fr, (k, side), side, f_send, f_recv).wait_send()
+            hop(ds, dr, (k, side), side, d_send, d_recv).wait_send()
+    for side in range(2):
+        hop(js, jr, (side,), side, j_send, j_recv).wait_send()
     all_of(rowbuf, n_flat - 1, 0).wait_send()
     all_of(colbuf, n_row - 1, 1).wait_send()
     all_of(totbuf, n_flat - 1, 2).wait_send()
+
+
+def apply(u_ref, step_ref, row_ref, col_ref, w_ref, ow_hbm, orow_hbm, ocol_hbm, nw, sem):
+    def out(i, a, b):
+        return pltpu.make_async_copy(a, b, sem.at[i])
+
+    small = [out(0, row_ref, orow_hbm), out(1, col_ref, ocol_hbm)]
+    for c in small:
+        c.start()
+    nw[...] = (w_ref[...].astype(jnp.float32) - step_ref[0:1, 0:1] * u_ref[...]).astype(jnp.bfloat16)
+    big = out(2, nw, ow_hbm)
+    big.start()
+    for c in small + [big]:
+        c.wait()
 
 
 def solution(mesh):
@@ -233,44 +246,53 @@
         cols = weights.shape[3]
         rc = rows // CHUNKS
         f32 = jnp.float32
+        keep = functools.partial(pltpu.with_memory_space_constraint, memory_space=pltpu.HBM)
         vmem = pl.BlockSpec(memory_space=pltpu.VMEM)
         hbm = pl.BlockSpec(memory_space=pltpu.HBM)
         dma = pltpu.SemaphoreType.DMA
         shapes = (
-            jax.ShapeDtypeStruct((rows, cols), jnp.bfloat16),
             jax.ShapeDtypeStruct((1, rows), f32),
             jax.ShapeDtypeStruct((1, cols), f32),
         )
-        new_w, row_moment, col_moment = pl.pallas_call(
+        update, step, row_moment, col_moment = pl.pallas_call(
             kernel,
-            out_shape=shapes,
-            in_specs=[hbm] * 5,
-            out_specs=(vmem,) * 3,
+            out_shape=(jax.ShapeDtypeStruct((rows, cols), f32), jax.ShapeDtypeStruct((1, LANES), f32)) + shapes,
+            in_specs=[hbm] * 4,
+            out_specs=(vmem,) * 4,
             scratch_shapes=[
                 pltpu.VMEM((2 * NX, rows, cols), jnp.bfloat16),
                 pltpu.VMEM((NX, rows, cols), f32),
                 pltpu.VMEM((NX, rows, cols), f32),
                 pltpu.VMEM((CHUNKS, 2, rc, cols // 2), f32),
                 pltpu.VMEM((CHUNKS, 2, rc, cols // 2), f32),
-                pltpu.VMEM((CHUNKS, 2, rc, cols), f32),
-                pltpu.VMEM((CHUNKS, 2, rc, cols), f32),
-                pltpu.VMEM((rows, cols), f32),
-                pltpu.VMEM((rows, cols), jnp.bfloat16),
+                pltpu.VMEM((2, rows, cols // 2), f32),
+                pltpu.VMEM((2, rows, cols // 2), f32),
+                pltpu.VMEM((CHUNKS, 2, rc, cols // 2), f32),
+                pltpu.VMEM((CHUNKS, 2, rc, cols // 2), f32),
                 pltpu.VMEM((1, rows), f32),
                 pltpu.VMEM((1, cols), f32),
                 pltpu.VMEM((1, 1), f32),
                 pltpu.VMEM((NX * NCORE * NZLO, 1, LANES), f32),
                 pltpu.VMEM((NY * NZHI, 8, LANES), f32),
                 pltpu.VMEM((NX * NCORE * NZLO, 1, LANES), f32),
-                dma((2 * NX,)), dma((4,)),
+                dma((2 * NX,)), dma((3,)),
                 dma((CHUNKS + 3,)), dma((CHUNKS + 3,)),
                 dma((CHUNKS, 2)), dma((CHUNKS, 2)),
+                dma((2,)), dma((2,)),
                 dma((CHUNKS, 2)), dma((CHUNKS, 2)),
                 dma((3,)), dma((3,)),
                 pltpu.SemaphoreType.REGULAR((4,)),
             ],
-            compiler_params=pltpu.CompilerParams(collective_id=0, has_side_effects=True, vmem_limit_bytes=63 << 20),
-        )(grad_parts.reshape(rows, width), weights.reshape(rows, cols), row_old, col_old.reshape(1, cols), step_rates.reshape(1, 1))
+            compiler_params=pltpu.CompilerParams(collective_id=0, has_side_effects=True, vmem_limit_bytes=32 << 20),
+        )(keep(grad_parts.reshape(rows, width)), keep(row_old), keep(col_old.reshape(1, cols)), step_rates.reshape(1, 1))
+        new_w, row_moment, col_moment = pl.pallas_call(
+            apply,
+            out_shape=(jax.ShapeDtypeStruct((rows, cols), jnp.bfloat16),) + shapes,
+            in_specs=[vmem] * 5,
+            out_specs=(pl.BlockSpec(memory_space=pl.ANY),) * 3,
+            scratch_shapes=[pltpu.VMEM((rows, cols), jnp.bfloat16), dma((3,))],
+            compiler_params=pltpu.CompilerParams(vmem_limit_bytes=4 << 20),
+        )(update, step, row_moment, col_moment, weights.reshape(rows, cols))
         return new_w.reshape(weights.shape), row_moment, col_moment.reshape(col_old.shape)
 
     in_specs = (

time: 52.9 us -> 49.6 us (0.938)
  local copies, waits for them, and re-layouts: 2.67 us -> 0.01 us
    unnamed x7 -> x2, local copies, waits for them, and re-layouts: 2.67 us -> 0.01 us
    pallas_call x1 -> x2, Pallas kernels: 48.7 us -> 48.2 us  [the longest x1 47.4 us: per_device(): pl.pallas_call(kernel, out_shape=(jax.ShapeDtypeStruct((rows, cols), f32)...]
where the time goes in v3:
time: 49.6 us; the launch traced here: 49.5 us
  Pallas kernels  48.2 us (97%)
  between operations  1.3 us (3%)
    pallas_call x1, Pallas kernels, per_device(): pl.pallas_call(kernel, out_shape=(jax.ShapeDtypeStruct((rows, cols), f32)...  47.4 us

profile of v3, /device:TPU:1, one launch (start us, length us, event | category | flops | bytes accessed | tf_op | source)
XLA Modules:
  0.0 49.5 jit_solution(3060680677131674757)
XLA Ops:
  1.3 0.0 copy-start
  1.3 47.4 %shard_map.76 = (f32[128,512]{1,0:T(8,128)S(1)}, f32[1,128]{1,0:T(1,128)S(1)}, f32[1,128]{1,0:T(1,128)S(1)}, f32[1,512]{1,0:T(1,128)S(1)}) custom-call(bf16[128,4096]{1,0:T(8,128)(2,1)} %bitcast.8, f32[1,128]{1,0:T(1,128)} %ro_hbm.1, f32[1,512]{1,0:T(1,128)} %bitcast.9, f32[1,1]{1,0:T(1,128)} %bitcast.6.sr_hbm), custom_call_target="tpu_custom_call" | custom-call | tf_op jit(solution)/shard_map/pallas_call | solution.py:257
  48.7 0.0 copy-done
  48.7 0.8 %shard_map.77 = (bf16[128,512]{1,0:T(8,128)(2,1)}, f32[1,128]{1,0:T(1,128)}, f32[1,512]{1,0:T(1,128)}) custom-call(f32[128,512]{1,0:T(8,128)S(1)} %get-tuple-element.10.u_ref, f32[1,128]{1,0:T(1,128)S(1)} %get-tuple-element.11.step_ref, f32[1,128]{1,0:T(1,128)S(1)} %get-tuple-element.12.row_ref, f32[1,512]{1,0:T(1,128)S(1)} %get-tuple-element.13.col_ref, ...), custom_call_target="tpu_custom_call" | custom-call | tf_op jit(solution)/shard_map/pallas_call | solution.py:288
Async XLA Ops:
  1.3 47.4 %copy-start = (bf16[1,128,1,512]{3,1,2,0:T(8,128)(2,1)S(1)}, bf16[1,128,1,512]{3,1,2,0:T(8,128)(2,1)}, u32[]{:S(2)}) copy-start(bf16[1,128,1,512]{3,1,2,0:T(8,128)(2,1)} %param.6) | copy-start | bytes 393220

commit v4 on v3

--- a/solution.py
+++ b/solution.py
@@ -63,8 +63,26 @@
     ]
 
     barrier = pltpu.get_barrier_semaphore()
-    for d in near:
+    for d in (at(dc=1), at(dx=1), at(dx=-1)):
         pl.semaphore_signal(barrier, inc=1, device_id=d, device_id_type=MESH)
+    greets = 3
+    answers = 0
+    replies = []
+    for place, size, up, down in ((z, NZ, at(dz=1), at(dz=-1)), (y, NY, at(dy=1), at(dy=-1))):
+        first, last = place == 0, place == size - 1
+        greets = greets + jnp.where(first, 0, 1) + jnp.where(last, 1, 0)
+        answers = answers + jnp.where(last, 0, 1) + jnp.where(first, 1, 0)
+        for ok, d in ((jnp.logical_not(last), up), (first, down)):
+            @pl.when(ok)
+            def _(d=d):
+                pl.semaphore_signal(barrier, inc=1, device_id=d, device_id_type=MESH)
+        replies += [(jnp.logical_not(first), down), (last, up)]
+
+    def reply():
+        for ok, d in replies:
+            @pl.when(ok)
+            def _(d=d):
+                pl.semaphore_signal(met.at[4], inc=1, device_id=d, device_id_type=MESH)
 
     def tell(s):
         for d in steps[s]:
@@ -118,12 +136,12 @@
         load(rel, 1).wait()
         snd[rel] = part(rel, 1, whole)
         if n == 0:
-            pl.semaphore_wait(barrier, len(near))
+            pl.semaphore_wait(barrier, greets)
+            reply()
             for i in range(CHUNKS):
                 core_copy(i).start()
         else:
             core_copy(CHUNKS + n - 1).start()
-    tell(0)
 
     load(2, 0).wait()
     for k in range(CHUNKS):
@@ -132,13 +150,18 @@
         for side in range(2):
             fs[k, side] = far[:, side * half:(side + 1) * half]
             hop(fs, fr, (k, side), side, f_send, f_recv).start()
-    hear(0)
-    tell(1)
+    @pl.when(answers > 0)
+    def _():
+        pl.semaphore_wait(met.at[4], answers)
+
+    tell(0)
     for side, rel in ((0, 1), (1, 3)):
         load(rel, 0).wait()
         core_copy(CHUNKS + side).wait_recv()
         js[side] = part(rel, 0, whole, 1 - side) + prt[rel, :, halves[1 - side]]
         hop(js, jr, (side,), side, j_send, j_recv).start()
+    hear(0)
+    tell(1)
     for k in range(CHUNKS):
         for side, rel in ((0, 1), (1, 3)):
             near_sum = part(rel, 0, chunk(k), side) + prt[rel, chunk(k), halves[side]]
@@ -208,11 +231,6 @@
     exchange(totbuf, me, flat_peers, 2)
     for q in range(groups):
         gf[:, lane(q)] = gf[:, lane(q)] * lax.rsqrt(ocol_ref[:, lane(q)])
-    all_of(totbuf, n_flat - 1, 2).wait_recv()
-    total = jnp.sum(jnp.sum(totbuf[...], axis=0), axis=1, keepdims=True)
-    clip = 1.0 / jnp.maximum(1.0, jnp.sqrt(total / (D * QKV)) / 0.2)
-    step_ref[...] = jnp.broadcast_to(sr[...] * clip, step_ref.shape)
-
     for i in range(n_core):
         core_copy(i).wait_send()
     for k in range(CHUNKS):
@@ -223,6 +241,10 @@
         hop(js, jr, (side,), side, j_send, j_recv).wait_send()
     all_of(rowbuf, n_flat - 1, 0).wait_send()
     all_of(colbuf, n_row - 1, 1).wait_send()
+    all_of(totbuf, n_flat - 1, 2).wait_recv()
+    total = jnp.sum(jnp.sum(totbuf[...], axis=0), axis=1, keepdims=True)
+    clip = 1.0 / jnp.maximum(1.0, jnp.sqrt(total / (D * QKV)) / 0.2)
+    step_ref[...] = jnp.broadcast_to(sr[...] * clip, step_ref.shape)
     all_of(totbuf, n_flat - 1, 2).wait_send()
 
 
@@ -281,7 +303,7 @@
                 dma((2,)), dma((2,)),
                 dma((CHUNKS, 2)), dma((CHUNKS, 2)),
                 dma((3,)), dma((3,)),
-                pltpu.SemaphoreType.REGULAR((4,)),
+                pltpu.SemaphoreType.REGULAR((5,)),
             ],
             compiler_params=pltpu.CompilerParams(collective_id=0, has_side_effects=True, vmem_limit_bytes=32 << 20),
         )(keep(grad_parts.reshape(rows, width)), keep(row_old), keep(col_old.reshape(1, cols)), step_rates.reshape(1, 1))

time: 49.6 us -> 49.6 us (level)
  no operation moved by 1% of the time
where the time goes in v4:
time: 49.6 us; the launch traced here: 49.5 us
  Pallas kernels  48.2 us (97%)
  between operations  1.3 us (3%)
    pallas_call x1, Pallas kernels, per_device(): pl.pallas_call(kernel, out_shape=(jax.ShapeDtypeStruct((rows, cols), f32)...  47.4 us

profile of v4, /device:TPU:1, one launch (start us, length us, event | category | flops | bytes accessed | tf_op | source)
XLA Modules:
  0.0 49.5 jit_solution(11309603339597172100)
XLA Ops:
  1.3 0.0 copy-start
  1.3 47.4 %shard_map.76 = (f32[128,512]{1,0:T(8,128)S(1)}, f32[1,128]{1,0:T(1,128)S(1)}, f32[1,128]{1,0:T(1,128)S(1)}, f32[1,512]{1,0:T(1,128)S(1)}) custom-call(bf16[128,4096]{1,0:T(8,128)(2,1)} %bitcast.8, f32[1,128]{1,0:T(1,128)} %ro_hbm.1, f32[1,512]{1,0:T(1,128)} %bitcast.9, f32[1,1]{1,0:T(1,128)} %bitcast.6.sr_hbm), custom_call_target="tpu_custom_call" | custom-call | tf_op jit(solution)/shard_map/pallas_call | solution.py:279
  48.7 0.0 copy-done
  48.7 0.8 %shard_map.77 = (bf16[128,512]{1,0:T(8,128)(2,1)}, f32[1,128]{1,0:T(1,128)}, f32[1,512]{1,0:T(1,128)}) custom-call(f32[128,512]{1,0:T(8,128)S(1)} %get-tuple-element.10.u_ref, f32[1,128]{1,0:T(1,128)S(1)} %get-tuple-element.11.step_ref, f32[1,128]{1,0:T(1,128)S(1)} %get-tuple-element.12.row_ref, f32[1,512]{1,0:T(1,128)S(1)} %get-tuple-element.13.col_ref, ...), custom_call_target="tpu_custom_call" | custom-call | tf_op jit(solution)/shard_map/pallas_call | solution.py:310
Async XLA Ops:
  1.3 47.4 %copy-start = (bf16[1,128,1,512]{3,1,2,0:T(8,128)(2,1)S(1)}, bf16[1,128,1,512]{3,1,2,0:T(8,128)(2,1)}, u32[]{:S(2)}) copy-start(bf16[1,128,1,512]{3,1,2,0:T(8,128)(2,1)} %param.6) | copy-start | bytes 393220
